TPU v7x, 32 devices: a whole 2x2x4 slice. The times are simulated.
32 devices in a mesh: dp: 8 (over z, y), seq: 4 (over x, core).
Axes of the slice: x: 2, y: 2, z: 4, core: 2. Of those that a mesh axis runs over, the one named last changes fastest.
Arguments:
- tokens: bfloat16 [8, 512, 1024], P('dp', 'seq'), may hold values from -6 to 6
- cache_keys: bfloat16 [8, 2048, 1024], P('dp', 'seq')
- cache_values: bfloat16 [8, 2048, 1024], P('dp', 'seq'), may hold values from -6 to 6
- qkv_weight: bfloat16 [1024, 3072], P(None, 'seq'), may hold values from -0.1875 to 0.1875
- qkv_bias: float32 [3072], replicated, may hold values from -3 to 3
- out_weight: bfloat16 [1024, 1024], P('seq', 'dp'), may hold values from -0.1875 to 0.1875
- out_bias: float32 [1024], replicated, may hold values from -3 to 3
- norm_gain: float32 [1024], replicated, may hold values from 0.1 to 1.9
- norm_bias: float32 [1024], replicated, may hold values from -3 to 3
- cached_len: int32 [8], replicated, may hold values from 0 to 2048, as said below
- span_len: int32 [8], replicated, may hold values from 1 to 512, as said below
- slot_request: int32 [8], replicated, may hold values from 0 to 7, each once
Outputs:
- normed: bfloat16 [8, 512, 1024], P('dp', 'seq')
Inputs may be any that keep to these rules, and one draw needn't show every extreme that they name: `cached_len`: some request has exactly 2048 cached positions. `span_len`: some request has exactly 512 new tokens in use. `slot_request`: each request names one slot.
All inputs are finite; a program needn't handle non-finite values.
Results may differ from a plain program's by a relative error of at most 0.0085.
Values may be sent and summed in bfloat16 or wider, within the bound.
A program may use at most 64 MiB of HBM per device.

v0:
```python
import jax
import jax.numpy as jnp
from jax import lax
from jax.sharding import PartitionSpec as P

D = 1024
HEADS = 16
HEAD_DIM = 64


neg_big = -1e30


def local(
    tokens,
    cache_keys,
    cache_values,
    qkv_weight,
    qkv_bias,
    out_weight,
    out_bias,
    norm_gain,
    norm_bias,
    cached_len,
    span_len,
    slot_request,
):
    seq_index = lax.axis_index("seq")
    dp_index = lax.axis_index("dp")
    groups = lax.axis_size("seq")
    request = slot_request[dp_index]
    cached = cached_len[request]
    filled = span_len[request]
    inputs = tokens[0]
    own_rows = inputs.shape[0]
    cache_rows = cache_keys.shape[1]
    all_rows = own_rows * groups
    scale = HEAD_DIM ** (-0.5)
    qkv_full = lax.all_gather(qkv_weight, "seq", axis=1, tiled=True)
    summed = jnp.dot(inputs, qkv_full, preferred_element_type=jnp.float32)
    projected = (summed + qkv_bias).astype(jnp.bfloat16)
    split = projected.reshape(own_rows, HEADS, 3, HEAD_DIM)
    own_queries = split[:, :, 0].reshape(own_rows, D)
    new_keys = split[:, :, 1].reshape(own_rows, D)
    new_values = split[:, :, 2].reshape(own_rows, D)
    all_queries = lax.all_gather(own_queries, "seq", axis=0, tiled=True)
    keys = jnp.concatenate([cache_keys[0], new_keys], 0)
    values = jnp.concatenate([cache_values[0], new_values], 0)
    positions = jnp.arange(all_rows)
    cache_pos = seq_index * cache_rows + jnp.arange(cache_rows)
    new_pos = seq_index * own_rows + jnp.arange(own_rows)
    live_cache = jnp.broadcast_to(cache_pos[None, :] < cached, (all_rows, cache_rows))
    live_new = (new_pos[None, :] <= positions[:, None]) & (new_pos[None, :] < filled)
    live = jnp.concatenate([live_cache, live_new], 1)

    def attend(head, carry):
        outputs, tops, totals = carry
        start = head * HEAD_DIM
        query = lax.dynamic_slice_in_dim(all_queries, start, HEAD_DIM, 1)
        key_block = lax.dynamic_slice_in_dim(keys, start, HEAD_DIM, 1)
        value_block = lax.dynamic_slice_in_dim(values, start, HEAD_DIM, 1)
        scores = (
            lax.dot_general(
                query, key_block, (((1,), (1,)), ((), ())), preferred_element_type=jnp.float32
            )
            * scale
        )
        masked = jnp.where(live, scores, neg_big)
        top = jnp.max(masked, axis=1)
        weights = jnp.where(live, jnp.exp(masked - top[:, None]), 0.0)
        total = jnp.sum(weights, axis=1)
        numer = jnp.dot(
            weights.astype(jnp.bfloat16), value_block, preferred_element_type=jnp.float32
        )
        result = (numer / jnp.maximum(total, 1.0)[:, None]).astype(jnp.bfloat16)
        outputs = lax.dynamic_update_slice_in_dim(outputs, result, start, 1)
        tops = lax.dynamic_update_slice(tops, top[:, None], (0, head))
        totals = lax.dynamic_update_slice(totals, total[:, None], (0, head))
        return (outputs, tops, totals)

    start_state = (
        jnp.zeros((all_rows, D), jnp.bfloat16),
        jnp.zeros((all_rows, HEADS), jnp.float32),
        jnp.zeros((all_rows, HEADS), jnp.float32),
    )
    partial_value, tops, totals = lax.fori_loop(0, HEADS, attend, start_state)
    partial_wide = partial_value.astype(jnp.float32)
    every_partial, every_top, every_total = (
        lax.all_gather(partial_wide[None], "seq", axis=0, tiled=True),
        lax.all_gather(tops[None], "seq", axis=0, tiled=True),
        lax.all_gather(totals[None], "seq", axis=0, tiled=True),
    )
    mine_partial = lax.dynamic_slice_in_dim(every_partial, seq_index * own_rows, own_rows, 1)
    mine_top = lax.dynamic_slice_in_dim(every_top, seq_index * own_rows, own_rows, 1)
    mine_total = lax.dynamic_slice_in_dim(every_total, seq_index * own_rows, own_rows, 1)
    best = jnp.max(mine_top, axis=0)
    share = mine_total * jnp.exp(mine_top - best[None])
    denom = jnp.sum(share, axis=0)
    spread_parts = mine_partial.reshape(groups, own_rows, HEADS, HEAD_DIM)
    attn = (
        (jnp.sum(share[:, :, :, None] * spread_parts, axis=0) / denom[:, :, None])
        .reshape(own_rows, D)
        .astype(jnp.bfloat16)
    )
    head_rows = lax.all_gather(out_weight, "dp", axis=1, tiled=True)
    out_full = lax.all_gather(head_rows, "seq", axis=0, tiled=True)
    projected_out = jnp.dot(attn, out_full, preferred_element_type=jnp.float32)
    mixed = projected_out + out_bias + inputs.astype(jnp.float32)
    center = mixed - jnp.mean(mixed, axis=1, keepdims=True)
    variance = jnp.mean(center * center, axis=1, keepdims=True)
    normed = (center * lax.rsqrt(variance + 1e-05) * norm_gain + norm_bias).astype(jnp.bfloat16)
    return normed[None]


def solution(mesh):
    return jax.shard_map(
        local,
        mesh=mesh,
        in_specs=(
            P("dp", "seq", None),
            P("dp", "seq", None),
            P("dp", "seq", None),
            P(None, "seq"),
            P(),
            P("seq", "dp"),
            P(),
            P(),
            P(),
            P(),
            P(),
            P(),
        ),
        out_specs=P("dp", "seq", None),
        check_vma=False,
    )
```

profile of v0, /device:TPU:0, one launch (start us, length us, event | category | flops | bytes accessed | tf_op | source)
XLA Modules:
  0.0 230.9 jit_solution(1036459860229054314)
XLA Ops:
  7.3 50.7 %all-gather.8.cloned.1.call-done = bf16[1024,3072]{1,0:T(8,128)(2,1)} async-done(((bf16[1024,768]{1,0:T(8,128)(2,1)}), bf16[1024,3072]{1,0:T(8,128)(2,1)}) %all-gather.8.cloned.1.call-update) | async-done | bytes 6291472 | tf_op jit(solution)/shard_map/all_gather | solution.py:39
  58.0 3.8 %fusion.15 = bf16[128,3072]{1,0:T(8,128)(2,1)S(1)} fusion(bf16[1024,3072]{1,0:T(8,128)(2,1)} %all-gather.8.cloned.1.call-done, f32[3072]{0:T(1024)S(1)} %copy-done.3, bf16[1,128,1024]{2,1,0:T(8,128)(2,1)S(1)} %copy-done), kind=kOutput, calls=%fused_computation.19 | convolution fusion | flops 806092800 | bytes 7352320 | tf_op jit(solution)/shard_map/dot_general | solution.py:40
  62.2 0.8 fusion.28
  68.4 2.6 %pad_maximum_fusion = (bf16[640,1024]{1,0:T(8,128)(2,1)S(1)}, bf16[640,1024]{1,0:T(8,128)(2,1)}) fusion(bf16[128,1024]{1,0:T(8,128)(2,1)S(1)} %copy.14, bf16[512,1024]{1,0:T(8,128)(2,1)S(1)} %bitcast.39, bf16[128,1024]{1,0:T(8,128)(2,1)S(1)} %copy.15, bf16[512,1024]{1,0:T(8,128)(2,1)} %bitcast.40), kind=kLoop, calls=%fused_computation.22 | loop fusion | flops 5242880 | bytes 5242880 | tf_op jit(solution)/shard_map/concatenate | solution.py:47
  71.0 9.1 %all-gather.10.cloned.1.call-done = bf16[512,1024]{0,1:T(8,128)(2,1)} async-done(((bf16[128,1024]{0,1:T(8,128)(2,1)}), bf16[512,1024]{0,1:T(8,128)(2,1)}) %all-gather.10.cloned.1.call-update) | async-done | bytes 1048592 | tf_op jit(solution)/shard_map/all_gather | solution.py:46
  80.1 55.4 %while.17 = (s32[]{:T(128)}, bf16[512,1024]{0,1:T(8,128)(2,1)S(1)}, f32[512,16]{0,1:T(8,128)S(1)}, f32[512,16]{0,1:T(8,128)S(1)}, bf16[512,1024]{0,1:T(8,128)(2,...) while((s32[]{:T(128)}, bf16[512,1024]{0,1:T(8,128)(2,1)S(1)}, ...), condition=%wide.region_3.4_spmd, body=%wide.region_0.3_spmd.sunk | while | flops 86900224 | bytes 5398699 | solution.py:86
  80.1 1.4 fusion.41
  82.0 1.4 fusion.43
  83.6 1.4 fusion.41
  85.5 1.4 fusion.43
  87.1 1.4 fusion.41
  88.9 1.4 fusion.43
  90.5 1.4 fusion.41
  92.4 1.4 fusion.43
  94.0 1.4 fusion.41
  95.9 1.4 fusion.43
  97.5 1.4 fusion.41
  99.3 1.4 fusion.43
  100.9 1.4 fusion.41
  102.8 1.4 fusion.43
  104.4 1.4 fusion.41
  106.3 1.4 fusion.43
  107.9 1.4 fusion.41
  109.7 1.4 fusion.43
  111.3 1.4 fusion.41
  113.2 1.4 fusion.43
  114.8 1.4 fusion.41
  116.7 1.4 fusion.43
  118.3 1.4 fusion.41
  120.1 1.4 fusion.43
  121.7 1.4 fusion.41
  123.6 1.4 fusion.43
  125.2 1.4 fusion.41
  127.1 1.4 fusion.43
  128.7 1.4 fusion.41
  130.5 1.4 fusion.43
  132.1 1.4 fusion.41
  134.0 1.4 fusion.43
  135.6 1.6 broadcast_in_dim.74
  138.1 28.5 %all_gather.26 = bf16[256,1024]{1,0:T(8,128)(2,1)} all-gather(bf16[256,128]{1,0:T(8,128)(2,1)S(1)} %copy-done.2), channel_id=1, replica_groups=mesh['dp'=8,'seq'=4] {'dp'}, dimensions={1}, use_global_device_ids=true | all-gather | bytes 589824 | tf_op jit(solution)/shard_map/all_gather | solution.py:105
  166.6 6.1 %all-gather = f32[2048,16]{0,1:T(8,128)S(1)} all-gather(f32[512,16]{0,1:T(8,128)S(1)} %get-tuple-element.146), channel_id=2, replica_groups=mesh['dp'=8,'seq'=4] {'seq'}, dimensions={0}, use_global_device_ids=true | all-gather | bytes 163840 | tf_op jit(solution)/shard_map/all_gather | solution.py:91
  172.8 6.2 %all-gather.1 = f32[2048,16]{0,1:T(8,128)S(1)} all-gather(f32[512,16]{0,1:T(8,128)S(1)} %get-tuple-element.147), channel_id=3, replica_groups=mesh['dp'=8,'seq'=4] {'seq'}, dimensions={0}, use_global_device_ids=true | all-gather | bytes 163840 | tf_op jit(solution)/shard_map/all_gather | solution.py:90
  179.1 17.9 %all-gather.14.cloned.1.call-done = f32[2048,1024]{0,1:T(8,128)} async-done(((f32[512,1024]{0,1:T(8,128)}), f32[2048,1024]{0,1:T(8,128)}) %all-gather.14.cloned.1.call-update) | async-done | bytes 8388624 | tf_op jit(solution)/shard_map/all_gather | solution.py:89
  197.1 10.9 %reshape.53 = f32[4,512,1024]{1,0,2:T(4,128)} reshape(f32[2048,1024]{0,1:T(8,128)} %all-gather.14.cloned.1.call-done) | data formatting | bytes 16777216 | tf_op jit(solution)/shard_map/all_gather | solution.py:89
  208.0 3.0 %fusion.16 = f32[128,1024]{0,1:T(8,128)S(1)} fusion(f32[4,512,1024]{1,0,2:T(4,128)} %reshape.53, s32[]{:T(128)S(6)} %select_n.45, f32[4,128,16]{1,0,2:T(4,128)S(1)} %get-tuple-element.179), kind=kLoop, calls=%fused_computation.21 | loop fusion | flops 917504 | bytes 2654212 | tf_op jit(solution)/shard_map/reduce_sum | solution.py:101
  211.1 10.1 %all-gather.12.cloned.1.call-done = bf16[1024,1024]{1,0:T(8,128)(2,1)} async-done(((bf16[256,1024]{1,0:T(8,128)(2,1)}), bf16[1024,1024]{1,0:T(8,128)(2,1)}) %all-gather.12.cloned.1.call-update) | async-done | bytes 2097168 | tf_op jit(solution)/shard_map/all_gather | solution.py:106
  221.1 2.1 fusion.30
  223.5 0.9 fusion.22
  (114 shorter events, 15.6 us)
Async XLA Ops:
  6.5 51.5 %copy-start = (bf16[1,128,1024]{2,1,0:T(8,128)(2,1)S(1)}, bf16[1,128,1024]{2,1,0:T(8,128)(2,1)}, u32[]{:S(2)}) copy-start(bf16[1,128,1024]{2,1,0:T(8,128)(2,1)} %param.14) | copy-start | bytes 786436
  6.5 51.5 %copy-start.3 = (f32[3072]{0:T(1024)S(1)}, f32[3072]{0:T(1024)}, u32[]{:S(2)}) copy-start(f32[3072]{0:T(1024)} %param.18) | copy-start | bytes 36868
  6.5 51.5 %all-gather.8.cloned.1.call-start = ((), (), s32[]{:S(2)}) async-start(), calls=%async_computation | async-start | bytes 7864320 | tf_op jit(solution)/shard_map/all_gather | solution.py:39
  7.3 72.8 %all-gather.10.cloned.1.call-start = ((), (), s32[]{:S(2)}) async-start(), calls=%async_computation.1 | async-start | bytes 1310720 | tf_op jit(solution)/shard_map/all_gather | solution.py:46
  62.2 0.9 copy-start.7
  62.2 3.2 %copy-start.8 = (s32[8]{0:T(128)S(1)}, s32[8]{0:T(128)}, u32[]{:S(2)}) copy-start(s32[8]{0:T(128)} %param.24) | copy-start | bytes 100
  62.2 3.7 %copy-start.9 = (s32[8]{0:T(128)S(1)}, s32[8]{0:T(128)}, u32[]{:S(2)}) copy-start(s32[8]{0:T(128)} %param.23) | copy-start | bytes 100
  63.0 5.4 %copy-start.1 = (bf16[1,512,1024]{2,1,0:T(8,128)(2,1)S(1)}, bf16[1,512,1024]{2,1,0:T(8,128)(2,1)}, u32[]{:S(2)}) copy-start(bf16[1,512,1024]{2,1,0:T(8,128)(2,1)} %param.15) | copy-start | bytes 3145732
  63.0 134.1 %all-gather.14.cloned.1.call-start = ((), (), s32[]{:S(2)}) async-start(), calls=%async_computation.3 | async-start | bytes 10485760 | tf_op jit(solution)/shard_map/all_gather | solution.py:89
  137.2 0.8 copy-start.2
  137.2 83.9 %all-gather.12.cloned.1.call-start = ((), (), s32[]{:S(2)}) async-start(), calls=%async_computation.2 | async-start | bytes 2621440 | tf_op jit(solution)/shard_map/all_gather | solution.py:106
  208.0 13.2 %copy-start.4 = (f32[1024]{0:T(1024)S(1)}, f32[1024]{0:T(1024)}, u32[]{:S(2)}) copy-start(f32[1024]{0:T(1024)} %param.20) | copy-start | bytes 12292
  211.1 12.4 %copy-start.5 = (f32[1024]{0:T(1024)S(1)}, f32[1024]{0:T(1024)}, u32[]{:S(2)}) copy-start(f32[1024]{0:T(1024)} %param.22) | copy-start | bytes 12292
  211.1 12.4 %copy-start.6 = (f32[1024]{0:T(1024)S(1)}, f32[1024]{0:T(1024)}, u32[]{:S(2)}) copy-start(f32[1024]{0:T(1024)} %param.21) | copy-start | bytes 12292
Sparse Core Ops, SparseCore 0:
  8.9 49.0 all-gather.7
  63.1 16.8 all-gather.9
  137.4 59.6 all-gather.13
  198.5 22.5 all-gather.11
where the time goes:
time: 233 us; the launch traced here: 231 us
  waiting for transfers between devices  88.6 us (38%)
  matrix products  51.2 us (22%)
  blocking collectives  40.8 us (18%)
  local copies, waits for them, and re-layouts  17.2 us (7%)
  other arithmetic  17.2 us (7%)
  between operations  15 us (6%)
    all_gather x1, waiting for transfers between devices, local(): qkv_full = lax.all_gather(qkv_weight, 'seq', axis=1, tiled=True)  50.7 us
    all_gather x1, blocking collectives, local(): head_rows = lax.all_gather(out_weight, 'dp', axis=1, tiled=True)  28.5 us
    dot_general x16, matrix products, attend(): jnp.dot(weights.astype(jnp.bfloat16), value_block, preferred_element_type...  22.8 us
    dot_general x16, matrix products, attend(): lax.dot_general(query, key_block, (((1,), (1,)), ((), ())), preferred_ele...  22.5 us
    all_gather x1, waiting for transfers between devices, local(): lax.all_gather(partial_wide[None], 'seq', axis=0, tiled=True)  17.9 us
    all_gather x1, local copies, waits for them, and re-layouts, local(): lax.all_gather(partial_wide[None], 'seq', axis=0, tiled=True)  10.9 us
    all_gather x1, waiting for transfers between devices, local(): out_full = lax.all_gather(head_rows, 'seq', axis=0, tiled=True)  10.1 us
    all_gather x1, waiting for transfers between devices, local(): all_queries = lax.all_gather(own_queries, 'seq', axis=0, tiled=True)  9.1 us
  transfers between devices with their start and end apart: 4, of which 4 were waited for; matrix products, arithmetic and copies ran while one was open for 9% of the time, Pallas kernels for 0%

commit v1 on v0

v1 whole, which is shorter than its diff:
```python
import functools

import jax
import jax.numpy as jnp
from jax import lax
from jax.experimental import pallas as pl
from jax.experimental.pallas import tpu as pltpu
from jax.sharding import PartitionSpec as P

HEAD_DIM = 64
LIVE = 3e38
DEAD = -1e30
F32 = jnp.float32
BF16 = jnp.bfloat16
MESH = pl.DeviceIdType.MESH


def peers():
    me = lax.axis_index("seq")
    core = me % 2
    partner = me + 1 - 2 * core
    twin = (me + 2) % 4
    diag = (partner + 2) % 4
    return me, core, partner, twin, diag


def greet(devices):
    barrier = pltpu.get_barrier_semaphore()
    for device in devices:
        pl.semaphore_signal(barrier, inc=1, device_id={"seq": device}, device_id_type=MESH)
    pl.semaphore_wait(barrier, len(devices))


def cols(index, width):
    return pl.ds(pl.multiple_of(index * width, 128), width)


def nt(a, b):
    return lax.dot_general(a, b, (((1,), (1,)), ((), ())), preferred_element_type=F32)


def attend(query, keys, caps, values, heads):
    rows, width = query.shape
    lane = lax.broadcasted_iota(jnp.int32, (rows, width), 1) // HEAD_DIM
    zero = jnp.zeros_like(query)
    stacked = jnp.concatenate([jnp.where(lane == h, query, zero) for h in range(heads)], 0)
    scores = [jnp.minimum(nt(stacked, k), cap) for k, cap in zip(keys, caps)]
    top = functools.reduce(jnp.maximum, [jnp.max(s, 1, keepdims=True) for s in scores])
    total, numer = 0.0, 0.0
    for s, v in zip(scores, values):
        weights = jnp.exp(s - top)
        total = total + jnp.sum(weights, 1, keepdims=True)
        numer = numer + jnp.dot(weights.astype(BF16), v, preferred_element_type=F32)
    return numer, top, total


def pick(stacked, rows, heads):
    width = heads * HEAD_DIM
    lane = lax.broadcasted_iota(jnp.int32, (rows, width), 1) // HEAD_DIM
    out = stacked[0:rows]
    for h in range(1, heads):
        out = jnp.where(lane == h, stacked[h * rows : (h + 1) * rows], out)
    return out


def stat_tile(top, total, rows, heads):
    lane = lax.broadcasted_iota(jnp.int32, (rows, 128), 1)
    out = jnp.ones((rows, 128), F32)
    for h in range(heads):
        out = jnp.where(lane == h, top[h * rows : (h + 1) * rows], out)
        out = jnp.where(lane == heads + h, total[h * rows : (h + 1) * rows], out)
    return out


def spread(tile, rows, heads):
    lane = lax.broadcasted_iota(jnp.int32, (rows, heads * HEAD_DIM), 1) // HEAD_DIM
    out = jnp.broadcast_to(tile[:, 0:1], (rows, heads * HEAD_DIM))
    for h in range(1, heads):
        out = jnp.where(lane == h, tile[:, h : h + 1], out)
    return out


def attention_kernel(
    cached_ref,
    span_ref,
    slot_ref,
    tokens_hbm,
    keys_hbm,
    values_hbm,
    weight_hbm,
    bias_ref,
    out_ref,
    tok,
    weight,
    kc,
    vc,
    kn,
    vn,
    qo,
    qt,
    numer_own,
    stat_own,
    part_send,
    part_recv,
    stat_send,
    stat_recv,
    attn,
    local_sem,
    tok_send,
    tok_recv,
    cache_send,
    cache_recv,
    q_send,
    q_recv,
    p_send,
    p_recv,
    a_send,
    a_recv,
):
    me, core, partner, twin, diag = peers()
    chip = me // 2
    rows = tok.shape[1]
    cache_rows = kc.shape[2]
    width = kc.shape[3]
    heads = width // HEAD_DIM
    request = slot_ref[lax.axis_index("dp")]
    cached = cached_ref[request]
    filled = span_ref[request]

    locals_ = [
        pltpu.make_async_copy(tokens_hbm.at[0], tok.at[me], local_sem.at[0]),
        pltpu.make_async_copy(weight_hbm, weight, local_sem.at[1]),
    ]
    for at, (hbm, buf) in enumerate(((keys_hbm, kc), (values_hbm, vc))):
        for group, owner in enumerate((me, twin)):
            locals_.append(
                pltpu.make_async_copy(
                    hbm.at[0, :, cols(owner, width)],
                    buf.at[group, core],
                    local_sem.at[2 + 2 * at + group],
                )
            )
    for copy in locals_:
        copy.start()

    greet((partner, twin))

    def remote(src, dst, send, recv, device):
        return pltpu.make_async_remote_copy(
            src_ref=src,
            dst_ref=dst,
            send_sem=send,
            recv_sem=recv,
            device_id={"seq": device},
            device_id_type=MESH,
        )

    to_twin = remote(tokens_hbm.at[0], tok.at[me], tok_send.at[1], tok_recv.at[1], twin)
    to_twin.start()
    to_partner = remote(tokens_hbm.at[0], tok.at[me], tok_send.at[0], tok_recv.at[0], partner)
    to_partner.start()
    forward = remote(tok.at[twin], tok.at[twin], tok_send.at[2], tok_recv.at[2], partner)
    cache_copies = []
    for at, (hbm, buf) in enumerate(((keys_hbm, kc), (values_hbm, vc))):
        for group, owner in enumerate((partner, diag)):
            cache_copies.append(
                remote(
                    hbm.at[0, :, cols(owner, width)],
                    buf.at[group, core],
                    cache_send.at[2 * at + group],
                    cache_recv.at[2 * at + group],
                    partner,
                )
            )
    for copy in cache_copies:
        copy.start()

    bias = bias_ref[:, cols(me, 3 * width)]
    low = lax.broadcasted_iota(jnp.int32, (rows, 128), 1) < HEAD_DIM

    def query_copy(block):
        return remote(qo.at[block], qt.at[block], q_send.at[block], q_recv.at[block], twin)

    def project(block):
        summed = jnp.dot(tok[block], weight[...], preferred_element_type=F32) + bias
        queries, keys, values = [], [], []
        for pair in range(heads // 2):
            a, b, c = (
                summed[:, (3 * pair + i) * 128 : (3 * pair + i + 1) * 128] for i in range(3)
            )
            queries.append(jnp.where(low, a, b))
            keys.append(pltpu.roll(jnp.where(low, c, a), HEAD_DIM, 1))
            values.append(jnp.where(low, b, c))
        scaled = jnp.concatenate(queries, 1).astype(BF16).astype(F32) * HEAD_DIM**-0.5
        qo[block] = scaled.astype(BF16)
        kn[block] = jnp.concatenate(keys, 1).astype(BF16)
        vn[block] = jnp.concatenate(values, 1).astype(BF16)
        query_copy(block).start()

    locals_[0].wait()
    locals_[1].wait()
    project(me)
    to_partner.wait_recv()
    project(partner)
    to_twin.wait_recv()
    forward.start()
    project(twin)
    forward.wait_recv()
    project(diag)

    for copy in locals_[2:]:
        copy.wait()
    for copy in cache_copies:
        copy.wait_recv()

    place = lax.broadcasted_iota(jnp.int32, (1, cache_rows), 1)
    caps = [
        jnp.where((2 * chip + j) * cache_rows + place < cached, LIVE, DEAD) for j in range(2)
    ]

    blocks = tok.shape[0]
    new_rows = blocks * rows
    for block in range(blocks):
        seen = (block + 1) * rows
        stacked_row = lax.broadcasted_iota(jnp.int32, (heads * rows, seen), 0) % rows
        new = lax.broadcasted_iota(jnp.int32, (heads * rows, seen), 1)
        alive = (new <= block * rows + stacked_row) & (new < filled)
        new_cap = jnp.where(alive, LIVE, DEAD)
        numer, top, total = attend(
            qo[block],
            [kc[0, 0], kc[0, 1], kn[0 : block + 1].reshape(seen, width)],
            caps + [new_cap],
            [vc[0, 0], vc[0, 1], vn[0 : block + 1].reshape(seen, width)],
            heads,
        )
        numer_own[block] = pick(numer, rows, heads)
        stat_own[block] = stat_tile(top, total, rows, heads)

    def part_copies(block):
        return (
            remote(
                part_send.at[block],
                part_recv.at[block],
                p_send.at[0, block],
                p_recv.at[0, block],
                twin,
            ),
            remote(
                stat_send.at[block],
                stat_recv.at[block],
                p_send.at[1, block],
                p_recv.at[1, block],
                twin,
            ),
        )

    def twin_block(block, carry):
        query_copy(block).wait_recv()
        numer, top, total = attend(
            qt[block], [kc[1, 0], kc[1, 1]], caps, [vc[1, 0], vc[1, 1]], heads
        )
        part_send[block] = pick(numer / total, rows, heads).astype(BF16)
        stat_send[block] = stat_tile(top, total, rows, heads).T[0 : 2 * heads]
        for copy in part_copies(block):
            copy.start()
        return carry

    lax.fori_loop(0, blocks, twin_block, 0)

    def combine(block, carry):
        for copy in part_copies(block):
            copy.wait_recv()
        other = jnp.concatenate(
            [stat_recv[block], jnp.ones((rows - 2 * heads, rows), F32)], 0
        ).T
        own = stat_own[block]
        best = jnp.maximum(own, other)
        scale_own = jnp.exp(own - best)
        scale_other = pltpu.roll(other, 128 - heads, 1) * jnp.exp(other - best)
        denom = pltpu.roll(own, 128 - heads, 1) * scale_own + scale_other
        mixed = numer_own[block] * spread(scale_own / denom, rows, heads)
        mixed = mixed + part_recv[block].astype(F32) * spread(scale_other / denom, rows, heads)
        attn[block] = mixed.astype(BF16)
        return carry

    lax.fori_loop(0, blocks, combine, 0)

    shared = [
        remote(attn.at[owner], out_ref.at[at, 1], a_send.at[at], a_recv.at[at], partner)
        for at, owner in enumerate((partner, diag))
    ]
    for copy in shared:
        copy.start()
    out_ref[0, 0] = attn[me]
    out_ref[1, 0] = attn[twin]
    for copy in shared:
        copy.wait()
    to_twin.wait_send()
    to_partner.wait_send()
    forward.wait_send()
    for copy in cache_copies:
        copy.wait_send()

    def drain(block, carry):
        query_copy(block).wait_send()
        for copy in part_copies(block):
            copy.wait_send()
        return carry

    lax.fori_loop(0, blocks, drain, 0)


def output_kernel(
    attn_ref, own_ref, other_ref, tokens_ref, bias_ref, gain_ref, shift_ref, out_ref, send, recv, s_sem, r_sem
):
    me, core, partner, twin, diag = peers()
    greet((twin,))

    def product(group):
        return jnp.dot(attn_ref[group, 0], own_ref[...], preferred_element_type=F32) + jnp.dot(
            attn_ref[group, 1], other_ref[...], preferred_element_type=F32
        )

    send[...] = product(1).astype(BF16)
    copy = pltpu.make_async_remote_copy(
        src_ref=send,
        dst_ref=recv,
        send_sem=s_sem,
        recv_sem=r_sem,
        device_id={"seq": twin},
        device_id_type=MESH,
    )
    copy.start()
    mixed = product(0) + bias_ref[...] + tokens_ref[0].astype(F32)
    copy.wait()
    mixed = mixed + recv[...].astype(F32)
    center = mixed - jnp.mean(mixed, axis=1, keepdims=True)
    variance = jnp.mean(center * center, axis=1, keepdims=True)
    normed = center * lax.rsqrt(variance + 1e-05) * gain_ref[...] + shift_ref[...]
    out_ref[0] = normed.astype(BF16)


def local(
    tokens,
    cache_keys,
    cache_values,
    qkv_weight,
    qkv_bias,
    out_weight,
    out_bias,
    norm_gain,
    norm_bias,
    cached_len,
    span_len,
    slot_request,
):
    rows, model = tokens.shape[1:]
    cache_rows = cache_keys.shape[1]
    width = qkv_weight.shape[1] // 3
    heads = width // HEAD_DIM
    blocks = lax.axis_size("seq")
    any_spec = pl.BlockSpec(memory_space=pl.ANY)
    vmem = pl.BlockSpec(memory_space=pltpu.VMEM)
    smem = pl.BlockSpec(memory_space=pltpu.SMEM)
    dma = pltpu.SemaphoreType.DMA

    own_weight = lax.all_gather(out_weight, "dp", axis=1, tiled=True)
    other_weight = lax.ppermute(own_weight, "seq", [(i, i ^ 1) for i in range(blocks)])

    attn = pl.pallas_call(
        attention_kernel,
        out_shape=jax.ShapeDtypeStruct((2, 2, rows, width), BF16),
        in_specs=[smem, smem, smem, any_spec, any_spec, any_spec, any_spec, vmem],
        out_specs=vmem,
        scratch_shapes=[
            pltpu.VMEM((blocks, rows, model), BF16),
            pltpu.VMEM((model, 3 * width), BF16),
            pltpu.VMEM((2, 2, cache_rows, width), BF16),
            pltpu.VMEM((2, 2, cache_rows, width), BF16),
            pltpu.VMEM((blocks, rows, width), BF16),
            pltpu.VMEM((blocks, rows, width), BF16),
            pltpu.VMEM((blocks, rows, width), BF16),
            pltpu.VMEM((blocks, rows, width), BF16),
            pltpu.VMEM((blocks, rows, width), F32),
            pltpu.VMEM((blocks, rows, 128), F32),
            pltpu.VMEM((blocks, rows, width), BF16),
            pltpu.VMEM((blocks, rows, width), BF16),
            pltpu.VMEM((blocks, 2 * heads, rows), F32),
            pltpu.VMEM((blocks, 2 * heads, rows), F32),
            pltpu.VMEM((blocks, rows, width), BF16),
            dma((6,)),
            dma((3,)),
            dma((3,)),
            dma((4,)),
            dma((4,)),
            dma((blocks,)),
            dma((blocks,)),
            dma((2, blocks)),
            dma((2, blocks)),
            dma((2,)),
            dma((2,)),
        ],
        compiler_params=pltpu.CompilerParams(
            collective_id=0, has_side_effects=True, vmem_limit_bytes=48 << 20
        ),
        cost_estimate=pl.CostEstimate(
            flops=6_000_000_000, bytes_accessed=6_000_000, transcendentals=5_000_000
        ),
        name="attention",
    )(
        cached_len,
        span_len,
        slot_request,
        tokens,
        cache_keys,
        cache_values,
        qkv_weight,
        qkv_bias.reshape(1, -1),
    )

    return pl.pallas_call(
        output_kernel,
        out_shape=jax.ShapeDtypeStruct((1, rows, model), BF16),
        in_specs=[vmem] * 7,
        out_specs=vmem,
        scratch_shapes=[
            pltpu.VMEM((rows, model), BF16),
            pltpu.VMEM((rows, model), BF16),
            dma,
            dma,
        ],
        compiler_params=pltpu.CompilerParams(
            collective_id=1, has_side_effects=True, vmem_limit_bytes=16 << 20
        ),
        cost_estimate=pl.CostEstimate(
            flops=300_000_000, bytes_accessed=2_000_000, transcendentals=0
        ),
        name="output",
    )(
        attn,
        own_weight,
        other_weight,
        tokens,
        out_bias.reshape(1, -1),
        norm_gain.reshape(1, -1),
        norm_bias.reshape(1, -1),
    )


def solution(mesh):
    return jax.shard_map(
        local,
        mesh=mesh,
        in_specs=(
            P("dp", "seq", None),
            P("dp", "seq", None),
            P("dp", "seq", None),
            P(None, "seq"),
            P(),
            P("seq", "dp"),
            P(),
            P(),
            P(),
            P(),
            P(),
            P(),
        ),
        out_specs=P("dp", "seq", None),
        check_vma=False,
    )
```

time: 233 us -> 75.3 us (0.32)
  waiting for transfers between devices: 88.6 us -> 0.01 us
  matrix products: 51.2 us -> 0 us
  Pallas kernels: 0 us -> 36.9 us
  other arithmetic: 17.2 us -> 0 us
  between operations: 15 us -> 0.06 us
  blocking collectives: 40.8 us -> 29.7 us
  local copies, waits for them, and re-layouts: 17.2 us -> 8.19 us
    all_gather x4 -> x0, waiting for transfers between devices: 87.8 us -> none  [the longest x1 50.7 us: local(): qkv_full = lax.all_gather(qkv_weight, 'seq', axis=1, tiled=True)]
    dot_general x34 -> x0, matrix products: 51.2 us -> none  [the longest x16 22.8 us: attend(): jnp.dot(weights.astype(jnp.bfloat16), value_block, preferred_element_type...]
    pallas_call x0 -> x2, Pallas kernels: none -> 36.9 us  [the longest x1 27.8 us: local(): pl.pallas_call(attention_kernel, out_shape=jax.ShapeDtypeStruct((2, 2, ro...]
    all_gather x3 -> x1, blocking collectives: 40.8 us -> 29.7 us  [local(): own_weight = lax.all_gather(out_weight, 'dp', axis=1, tiled=True)]
    all_gather x3 -> x0, local copies, waits for them, and re-layouts: 11.1 us -> none  [the longest x1 10.9 us: local(): lax.all_gather(partial_wide[None], 'seq', axis=0, tiled=True)]
    reduce_sum x18 -> x0, other arithmetic: 10.5 us -> none  [the longest x16 7.31 us: attend(): total = jnp.sum(weights, axis=1)]
    unnamed x20 -> x23, local copies, waits for them, and re-layouts: 0.81 us -> 8.19 us
    concatenate x2 -> x0, other arithmetic: 2.67 us -> none  [the longest x1 2.57 us: local(): keys = jnp.concatenate([cache_keys[0], new_keys], 0)]
  transfers between devices with their start and end apart: 4 -> 1, of which waited for: 4 -> 0; matrix products, arithmetic and copies ran while one was open for 9% -> 0% of each run, Pallas kernels for 0% -> 37%
where the time goes in v1:
time: 75.3 us; the launch traced here: 74.9 us
  Pallas kernels  36.9 us (49%)
  blocking collectives  29.7 us (39%)
  local copies, waits for them, and re-layouts  8.19 us (11%)
    all_gather x1, blocking collectives, local(): own_weight = lax.all_gather(out_weight, 'dp', axis=1, tiled=True)  29.7 us
    pallas_call x1, Pallas kernels, local(): pl.pallas_call(attention_kernel, out_shape=jax.ShapeDtypeStruct((2, 2, ro...  27.8 us
    pallas_call x1, Pallas kernels, local(): pl.pallas_call(output_kernel, out_shape=jax.ShapeDtypeStruct((1, rows, mo...  9.17 us
    unnamed x23, local copies, waits for them, and re-layouts  8.19 us
  transfers between devices with their start and end apart: 1, of which 0 were waited for; matrix products, arithmetic and copies ran while one was open for 0% of the time, Pallas kernels for 37%

profile of v1, /device:TPU:0, one launch (start us, length us, event | category | flops | bytes accessed | tf_op | source)
XLA Modules:
  0.0 74.9 jit_solution(8513475139763794535)
XLA Ops:
  0.0 29.7 %all_gather.3.own_ref = bf16[256,1024]{1,0:T(8,128)(2,1)S(1)} all-gather(bf16[256,128]{1,0:T(8,128)(2,1)} %param.17), channel_id=1, replica_groups=mesh['dp'=8,'seq'=4] {'dp'}, dimensions={1}, use_global_device_ids=true | all-gather | bytes 589824 | tf_op jit(solution)/shard_map/all_gather | solution.py:367
  29.7 0.0 collective-permute-start
  29.7 0.0 copy-start
  29.7 0.9 %copy-done = bf16[1,128,1024]{2,1,0:T(8,128)(2,1)S(1)} copy-done((bf16[1,128,1024]{2,1,0:T(8,128)(2,1)S(1)}, bf16[1,128,1024]{2,1,0:T(8,128)(2,1)}, u32[]{:S(2)}) %copy-start) | copy-done | bytes 262168
  30.7 0.0 copy-start.4
  30.7 1.4 %copy-done.4 = bf16[1024,768]{1,0:T(8,128)(2,1)S(1)} copy-done((bf16[1024,768]{1,0:T(8,128)(2,1)S(1)}, bf16[1024,768]{1,0:T(8,128)(2,1)}, u32[]{:S(2)}) %copy-start.4) | copy-done | bytes 1572888
  32.1 0.0 copy-start.5
  32.1 1.2 %copy-done.5 = bf16[1,512,1024]{2,1,0:T(8,128)(2,1)S(1)} copy-done((bf16[1,512,1024]{2,1,0:T(8,128)(2,1)S(1)}, bf16[1,512,1024]{2,1,0:T(8,128)(2,1)}, u32[]{:S(2)}) %copy-start.5) | copy-done | bytes 1048600
  33.3 0.0 copy-start.6
  33.3 1.2 %copy-done.6 = bf16[1,512,1024]{2,1,0:T(8,128)(2,1)S(1)} copy-done((bf16[1,512,1024]{2,1,0:T(8,128)(2,1)S(1)}, bf16[1,512,1024]{2,1,0:T(8,128)(2,1)}, u32[]{:S(2)}) %copy-start.6) | copy-done | bytes 1048600
  34.6 0.0 copy-start.7
  34.6 0.7 copy-done.7
  35.3 0.0 copy-start.8
  35.3 0.7 copy-done.8
  35.9 0.0 copy-start.9
  35.9 0.7 copy-done.9
  36.6 0.0 copy-start.10
  36.6 0.7 copy-done.10
  37.2 0.0 copy-start.1
  37.2 0.0 copy-start.2
  37.2 0.0 copy-start.3
  37.2 27.8 %attention.1.attn_ref = bf16[2,2,128,256]{3,2,1,0:T(8,128)(2,1)S(1)} custom-call(s32[8]{0:T(128)S(1)} %copy-done.8, s32[8]{0:T(128)S(1)} %copy-done.9, s32[8]{0:T(128)S(1)} %copy-done.10, bf16[1,128,1024]{2,1,0:T(8,128)(2,1)S(1)} %copy-done, bf16[1,512,1024]{2,1,0:T(8,128)(2,1)S(1)} %copy-done.5, bf16[1,512,1024]{2,1,0:T(8,128)(2,1)S(1)} %copy-done.6, ...), custom_call_target="tpu_custom_call" | custom-call | flops 6000000000 | bytes 6000000 | tf_op jit(solution)/shard_map/attention/pallas_call | solution.py:370
  65.0 0.0 collective-permute-done.other_ref
  65.0 0.0 copy-done.1
  65.0 0.0 copy-done.2
  65.0 0.0 copy-done.3
  65.0 9.2 %output.1 = bf16[1,128,1024]{2,1,0:T(8,128)(2,1)S(1)} custom-call(bf16[2,2,128,256]{3,2,1,0:T(8,128)(2,1)S(1)} %attention.1.attn_ref, bf16[256,1024]{1,0:T(8,128)(2,1)S(1)} %all_gather.3.own_ref, bf16[256,1024]{1,0:T(8,128)(2,1)S(1)} %collective-permute-done.other_ref, bf16[1,128,1024]{2,1,0:T(8,128)(2,1)S(1)} %copy-done, f32[1,1024]{1,0:T(1,128)S(1)} %bitcast.4, ...), custom_call_target="tpu_custom_call" | custom-call | flops 300000000 | bytes 2000000 | tf_op jit(solution)/shard_map/output/pallas_call | solution.py:421
  74.2 0.7 copy.14
Async XLA Ops:
  29.7 35.3 %collective-permute-start = (bf16[256,1024]{1,0:T(8,128)(2,1)S(1)}, bf16[256,1024]{1,0:T(8,128)(2,1)S(1)}, u32[]{:S(2)}, u32[]{:S(2)}) collective-permute-start(bf16[256,1024]{1,0:T(8,128)(2,1)S(1)} %all_gather.3.own_ref), channel_id=1, source_target_pairs={{0,1},{1,0},{2,3},{3,2},{4,5},{5,4},{6,7},{7,6},{8,9},{9,8},{10,11... | collective-permute-start | bytes 1572872 | tf_op jit(solution)/shard_map/ppermute | solution.py:368
  29.7 1.0 %copy-start = (bf16[1,128,1024]{2,1,0:T(8,128)(2,1)S(1)}, bf16[1,128,1024]{2,1,0:T(8,128)(2,1)}, u32[]{:S(2)}) copy-start(bf16[1,128,1024]{2,1,0:T(8,128)(2,1)} %tokens_ref.1) | copy-start | bytes 786436
  30.7 1.4 %copy-start.4 = (bf16[1024,768]{1,0:T(8,128)(2,1)S(1)}, bf16[1024,768]{1,0:T(8,128)(2,1)}, u32[]{:S(2)}) copy-start(bf16[1024,768]{1,0:T(8,128)(2,1)} %weight_hbm.1) | copy-start | bytes 4718596
  32.1 1.2 %copy-start.5 = (bf16[1,512,1024]{2,1,0:T(8,128)(2,1)S(1)}, bf16[1,512,1024]{2,1,0:T(8,128)(2,1)}, u32[]{:S(2)}) copy-start(bf16[1,512,1024]{2,1,0:T(8,128)(2,1)} %keys_hbm.1) | copy-start | bytes 3145732
  33.3 1.2 %copy-start.6 = (bf16[1,512,1024]{2,1,0:T(8,128)(2,1)S(1)}, bf16[1,512,1024]{2,1,0:T(8,128)(2,1)}, u32[]{:S(2)}) copy-start(bf16[1,512,1024]{2,1,0:T(8,128)(2,1)} %values_hbm.1) | copy-start | bytes 3145732
  34.6 0.7 copy-start.7
  35.3 0.7 copy-start.8
  35.9 0.7 copy-start.9
  36.6 0.7 copy-start.10
  37.2 27.8 %copy-start.1 = (f32[1024]{0:T(1024)S(1)}, f32[1024]{0:T(1024)}, u32[]{:S(2)}) copy-start(f32[1024]{0:T(1024)} %param.18) | copy-start | bytes 12292
  37.2 27.8 %copy-start.2 = (f32[1024]{0:T(1024)S(1)}, f32[1024]{0:T(1024)}, u32[]{:S(2)}) copy-start(f32[1024]{0:T(1024)} %param.19) | copy-start | bytes 12292
  37.2 27.8 %copy-start.3 = (f32[1024]{0:T(1024)S(1)}, f32[1024]{0:T(1024)}, u32[]{:S(2)}) copy-start(f32[1024]{0:T(1024)} %param.20) | copy-start | bytes 12292

commit v2 on v1

--- a/solution.py
+++ b/solution.py
@@ -22,13 +22,6 @@
     twin = (me + 2) % 4
     diag = (partner + 2) % 4
     return me, core, partner, twin, diag
-
-
-def greet(devices):
-    barrier = pltpu.get_barrier_semaphore()
-    for device in devices:
-        pl.semaphore_signal(barrier, inc=1, device_id={"seq": device}, device_id_type=MESH)
-    pl.semaphore_wait(barrier, len(devices))
 
 
 def cols(index, width):
@@ -80,7 +73,8 @@
     return out
 
 
-def attention_kernel(
+def kernel(
+    gather,
     cached_ref,
     span_ref,
     slot_ref,
@@ -88,7 +82,11 @@
     keys_hbm,
     values_hbm,
     weight_hbm,
+    out_weight_hbm,
     bias_ref,
+    out_bias_ref,
+    gain_ref,
+    shift_ref,
     out_ref,
     tok,
     weight,
@@ -105,6 +103,11 @@
     stat_send,
     stat_recv,
     attn,
+    other_attn,
+    wo,
+    other_wo,
+    y_send,
+    y_recv,
     local_sem,
     tok_send,
     tok_recv,
@@ -116,6 +119,11 @@
     p_recv,
     a_send,
     a_recv,
+    w_send,
+    w_recv,
+    f_sem,
+    ys_sem,
+    yr_sem,
 ):
     me, core, partner, twin, diag = peers()
     chip = me // 2
@@ -140,10 +148,24 @@
                     local_sem.at[2 + 2 * at + group],
                 )
             )
+    dp = lax.axis_index("dp")
+    parts = lax.axis_size("dp")
+    if gather:
+        piece = out_weight_hbm.shape[1]
+        mine = wo.at[:, cols(dp, piece)]
+    else:
+        mine = wo
+    own_weight = pltpu.make_async_copy(out_weight_hbm, mine, local_sem.at[6])
     for copy in locals_:
         copy.start()
-
-    greet((partner, twin))
+    own_weight.start()
+
+    barrier = pltpu.get_barrier_semaphore()
+    near = [{"seq": partner}, {"seq": twin}]
+    far = [{"dp": (dp + k) % parts} for k in range(1, parts)] if gather else []
+    for device in near + far:
+        pl.semaphore_signal(barrier, inc=1, device_id=device, device_id_type=MESH)
+    pl.semaphore_wait(barrier, len(near + far))
 
     def remote(src, dst, send, recv, device):
         return pltpu.make_async_remote_copy(
@@ -174,6 +196,19 @@
             )
     for copy in cache_copies:
         copy.start()
+    weight_copies = [
+        pltpu.make_async_remote_copy(
+            src_ref=out_weight_hbm,
+            dst_ref=mine,
+            send_sem=w_send.at[k],
+            recv_sem=w_recv.at[k],
+            device_id=device,
+            device_id_type=MESH,
+        )
+        for k, device in enumerate(far)
+    ]
+    for copy in weight_copies:
+        copy.start()
 
     bias = bias_ref[:, cols(me, 3 * width)]
     low = lax.broadcasted_iota(jnp.int32, (rows, 128), 1) < HEAD_DIM
@@ -236,6 +271,12 @@
         numer_own[block] = pick(numer, rows, heads)
         stat_own[block] = stat_tile(top, total, rows, heads)
 
+    own_weight.wait()
+    for copy in weight_copies:
+        copy.wait_recv()
+    share_weight = remote(wo, other_wo, f_sem.at[0], f_sem.at[1], partner)
+    share_weight.start()
+
     def part_copies(block):
         return (
             remote(
@@ -254,7 +295,8 @@
             ),
         )
 
-    def twin_block(block, carry):
+    def twin_block(step, carry):
+        block = 2 * ((chip + step // 2) % 2) + (core + step // 2 + step + 1) % 2
         query_copy(block).wait_recv()
         numer, top, total = attend(
             qt[block], [kc[1, 0], kc[1, 1]], caps, [vc[1, 0], vc[1, 1]], heads
@@ -265,9 +307,7 @@
             copy.start()
         return carry
 
-    lax.fori_loop(0, blocks, twin_block, 0)
-
-    def combine(block, carry):
+    def combine(block):
         for copy in part_copies(block):
             copy.wait_recv()
         other = jnp.concatenate(
@@ -281,24 +321,53 @@
         mixed = numer_own[block] * spread(scale_own / denom, rows, heads)
         mixed = mixed + part_recv[block].astype(F32) * spread(scale_other / denom, rows, heads)
         attn[block] = mixed.astype(BF16)
-        return carry
-
-    lax.fori_loop(0, blocks, combine, 0)
 
     shared = [
-        remote(attn.at[owner], out_ref.at[at, 1], a_send.at[at], a_recv.at[at], partner)
+        remote(attn.at[owner], other_attn.at[at], a_send.at[at], a_recv.at[at], partner)
         for at, owner in enumerate((partner, diag))
     ]
-    for copy in shared:
-        copy.start()
-    out_ref[0, 0] = attn[me]
-    out_ref[1, 0] = attn[twin]
-    for copy in shared:
-        copy.wait()
-    to_twin.wait_send()
-    to_partner.wait_send()
-    forward.wait_send()
-    for copy in cache_copies:
+    pieces, _, span = y_send.shape
+
+    def product(block, at, piece):
+        here = slice(piece * span, (piece + 1) * span)
+        return jnp.dot(attn[block], wo[:, here], preferred_element_type=F32) + jnp.dot(
+            other_attn[at], other_wo[:, here], preferred_element_type=F32
+        )
+
+    y_copies = [
+        remote(y_send.at[i], y_recv.at[i], ys_sem.at[i], yr_sem.at[i], twin)
+        for i in range(pieces)
+    ]
+
+    lax.fori_loop(0, blocks - 1, twin_block, 0)
+    combine(diag)
+    shared[1].start()
+    combine(twin)
+    twin_block(blocks - 1, 0)
+    share_weight.wait_recv()
+    shared[1].wait_recv()
+    for i in range(pieces):
+        y_send[i] = product(twin, 1, i).astype(BF16)
+        y_copies[i].start()
+    combine(partner)
+    shared[0].start()
+    combine(me)
+    shared[0].wait_recv()
+    mixed = [product(me, 0, i) for i in range(pieces)]
+    for i in range(pieces):
+        y_copies[i].wait_recv()
+    mixed = jnp.concatenate(
+        [mixed[i] + y_recv[i].astype(F32) for i in range(pieces)], 1
+    )
+    mixed = mixed + out_bias_ref[...] + tok[me].astype(F32)
+    center = mixed - jnp.mean(mixed, axis=1, keepdims=True)
+    variance = jnp.mean(center * center, axis=1, keepdims=True)
+    normed = center * lax.rsqrt(variance + 1e-05) * gain_ref[...] + shift_ref[...]
+    out_ref[0] = normed.astype(BF16)
+
+    for copy in [to_twin, to_partner, forward, share_weight]:
+        copy.wait_send()
+    for copy in cache_copies + weight_copies + shared + y_copies:
         copy.wait_send()
 
     def drain(block, carry):
@@ -308,36 +377,6 @@
         return carry
 
     lax.fori_loop(0, blocks, drain, 0)
-
-
-def output_kernel(
-    attn_ref, own_ref, other_ref, tokens_ref, bias_ref, gain_ref, shift_ref, out_ref, send, recv, s_sem, r_sem
-):
-    me, core, partner, twin, diag = peers()
-    greet((twin,))
-
-    def product(group):
-        return jnp.dot(attn_ref[group, 0], own_ref[...], preferred_element_type=F32) + jnp.dot(
-            attn_ref[group, 1], other_ref[...], preferred_element_type=F32
-        )
-
-    send[...] = product(1).astype(BF16)
-    copy = pltpu.make_async_remote_copy(
-        src_ref=send,
-        dst_ref=recv,
-        send_sem=s_sem,
-        recv_sem=r_sem,
-        device_id={"seq": twin},
-        device_id_type=MESH,
-    )
-    copy.start()
-    mixed = product(0) + bias_ref[...] + tokens_ref[0].astype(F32)
-    copy.wait()
-    mixed = mixed + recv[...].astype(F32)
-    center = mixed - jnp.mean(mixed, axis=1, keepdims=True)
-    variance = jnp.mean(center * center, axis=1, keepdims=True)
-    normed = center * lax.rsqrt(variance + 1e-05) * gain_ref[...] + shift_ref[...]
-    out_ref[0] = normed.astype(BF16)
 
 
 def local(
@@ -359,36 +398,47 @@
     width = qkv_weight.shape[1] // 3
     heads = width // HEAD_DIM
     blocks = lax.axis_size("seq")
-    any_spec = pl.BlockSpec(memory_space=pl.ANY)
+    hbm = pl.BlockSpec(memory_space=pltpu.HBM)
     vmem = pl.BlockSpec(memory_space=pltpu.VMEM)
     smem = pl.BlockSpec(memory_space=pltpu.SMEM)
     dma = pltpu.SemaphoreType.DMA
 
-    own_weight = lax.all_gather(out_weight, "dp", axis=1, tiled=True)
-    other_weight = lax.ppermute(own_weight, "seq", [(i, i ^ 1) for i in range(blocks)])
-
-    attn = pl.pallas_call(
-        attention_kernel,
-        out_shape=jax.ShapeDtypeStruct((2, 2, rows, width), BF16),
-        in_specs=[smem, smem, smem, any_spec, any_spec, any_spec, any_spec, vmem],
+    gather = out_weight.shape[1] % 128 == 0
+    if not gather:
+        out_weight = lax.all_gather(out_weight, "dp", axis=1, tiled=True)
+    far = lax.axis_size("dp") - 1 if gather else 1
+    pieces = 4
+
+    def half(count):
+        return pltpu.VMEM((count, rows, width), BF16)
+
+    return pl.pallas_call(
+        functools.partial(kernel, gather),
+        out_shape=jax.ShapeDtypeStruct((1, rows, model), BF16),
+        in_specs=[smem] * 3 + [hbm] * 5 + [vmem] * 4,
         out_specs=vmem,
         scratch_shapes=[
             pltpu.VMEM((blocks, rows, model), BF16),
             pltpu.VMEM((model, 3 * width), BF16),
             pltpu.VMEM((2, 2, cache_rows, width), BF16),
             pltpu.VMEM((2, 2, cache_rows, width), BF16),
-            pltpu.VMEM((blocks, rows, width), BF16),
-            pltpu.VMEM((blocks, rows, width), BF16),
-            pltpu.VMEM((blocks, rows, width), BF16),
-            pltpu.VMEM((blocks, rows, width), BF16),
+            half(blocks),
+            half(blocks),
+            half(blocks),
+            half(blocks),
             pltpu.VMEM((blocks, rows, width), F32),
             pltpu.VMEM((blocks, rows, 128), F32),
-            pltpu.VMEM((blocks, rows, width), BF16),
-            pltpu.VMEM((blocks, rows, width), BF16),
+            half(blocks),
+            half(blocks),
             pltpu.VMEM((blocks, 2 * heads, rows), F32),
             pltpu.VMEM((blocks, 2 * heads, rows), F32),
-            pltpu.VMEM((blocks, rows, width), BF16),
-            dma((6,)),
+            half(blocks),
+            half(2),
+            pltpu.VMEM((width, model), BF16),
+            pltpu.VMEM((width, model), BF16),
+            pltpu.VMEM((pieces, rows, model // pieces), BF16),
+            pltpu.VMEM((pieces, rows, model // pieces), BF16),
+            dma((7,)),
             dma((3,)),
             dma((3,)),
             dma((4,)),
@@ -399,14 +449,19 @@
             dma((2, blocks)),
             dma((2,)),
             dma((2,)),
+            dma((far,)),
+            dma((far,)),
+            dma((2,)),
+            dma((pieces,)),
+            dma((pieces,)),
         ],
         compiler_params=pltpu.CompilerParams(
-            collective_id=0, has_side_effects=True, vmem_limit_bytes=48 << 20
+            collective_id=0, has_side_effects=True, vmem_limit_bytes=60 << 20
         ),
         cost_estimate=pl.CostEstimate(
             flops=6_000_000_000, bytes_accessed=6_000_000, transcendentals=5_000_000
         ),
-        name="attention",
+        name="sublayer",
     )(
         cached_len,
         span_len,
@@ -415,32 +470,8 @@
         cache_keys,
         cache_values,
         qkv_weight,
+        out_weight,
         qkv_bias.reshape(1, -1),
-    )
-
-    return pl.pallas_call(
-        output_kernel,
-        out_shape=jax.ShapeDtypeStruct((1, rows, model), BF16),
-        in_specs=[vmem] * 7,
-        out_specs=vmem,
-        scratch_shapes=[
-            pltpu.VMEM((rows, model), BF16),
-            pltpu.VMEM((rows, model), BF16),
-            dma,
-            dma,
-        ],
-        compiler_params=pltpu.CompilerParams(
-            collective_id=1, has_side_effects=True, vmem_limit_bytes=16 << 20
-        ),
-        cost_estimate=pl.CostEstimate(
-            flops=300_000_000, bytes_accessed=2_000_000, transcendentals=0
-        ),
-        name="output",
-    )(
-        attn,
-        own_weight,
-        other_weight,
-        tokens,
         out_bias.reshape(1, -1),
         norm_gain.reshape(1, -1),
         norm_bias.reshape(1, -1),

time: 75.3 us -> 42.6 us (0.57)
  blocking collectives: 29.7 us -> 0 us
  local copies, waits for them, and re-layouts: 8.19 us -> 1.67 us
  Pallas kernels: 36.9 us -> 40.7 us
    all_gather x1 -> x0, blocking collectives: 29.7 us -> none  [local(): own_weight = lax.all_gather(out_weight, 'dp', axis=1, tiled=True)]
    unnamed x23 -> x1, local copies, waits for them, and re-layouts: 8.19 us -> 1.67 us
    pallas_call x2 -> x1, Pallas kernels: 36.9 us -> 40.7 us  [local(): pl.pallas_call(functools.partial(kernel, gather), out_shape=jax.ShapeDtyp...]
  transfers between devices with their start and end apart: 1 -> 0, of which waited for: 0 -> 0; matrix products, arithmetic and copies ran while one was open for 0% -> 0% of each run, Pallas kernels for 37% -> 0%
where the time goes in v2:
time: 42.6 us; the launch traced here: 42.4 us
  Pallas kernels  40.7 us (96%)
  local copies, waits for them, and re-layouts  1.67 us (4%)
    pallas_call x1, Pallas kernels, local(): pl.pallas_call(functools.partial(kernel, gather), out_shape=jax.ShapeDtyp...  40.7 us
    unnamed x1, local copies, waits for them, and re-layouts  1.67 us

profile of v2, /device:TPU:0, one launch (start us, length us, event | category | flops | bytes accessed | tf_op | source)
XLA Modules:
  0.0 42.4 jit_solution(13538581666129124910)
XLA Ops:
  0.0 40.7 %sublayer.1 = bf16[1,128,1024]{2,1,0:T(8,128)(2,1)} custom-call(s32[8]{0:T(128)} %cached_ref.1, s32[8]{0:T(128)} %span_ref.1, s32[8]{0:T(128)} %slot_ref.1, bf16[1,128,1024]{2,1,0:T(8,128)(2,1)} %tokens_hbm.1, bf16[1,512,1024]{2,1,0:T(8,128)(2,1)} %keys_hbm.1, bf16[1,512,1024]{2,1,0:T(8,128)(2,1)} %values_hbm.1, bf16[1024,768]{1,0:T(8,128)(2,1)} %weight_hbm.1, ...), custom_call_target="tpu_custom_call" | custom-call | flops 6000000000 | bytes 6000000 | tf_op jit(solution)/shard_map/sublayer/pallas_call | solution.py:415
  40.7 1.7 %copy.14 = bf16[1,128,1024]{2,1,0:T(8,128)(2,1)} copy(bf16[1,128,1024]{2,1,0:T(8,128)(2,1)} %sublayer.1) | data formatting | bytes 524288

commit v3 on v2

--- a/solution.py
+++ b/solution.py
@@ -96,8 +96,8 @@
     vn,
     qo,
     qt,
-    numer_own,
-    stat_own,
+    numer_keep,
+    stat_keep,
     part_send,
     part_recv,
     stat_send,
@@ -105,9 +105,6 @@
     attn,
     other_attn,
     wo,
-    other_wo,
-    y_send,
-    y_recv,
     local_sem,
     tok_send,
     tok_recv,
@@ -122,8 +119,7 @@
     w_send,
     w_recv,
     f_sem,
-    ys_sem,
-    yr_sem,
+    g_sem,
 ):
     me, core, partner, twin, diag = peers()
     chip = me // 2
@@ -152,7 +148,8 @@
     parts = lax.axis_size("dp")
     if gather:
         piece = out_weight_hbm.shape[1]
-        mine = wo.at[:, cols(dp, piece)]
+        mine = wo.at[me, :, cols(dp, piece)]
+        theirs = wo.at[twin, :, cols(dp, piece)]
     else:
         mine = wo
     own_weight = pltpu.make_async_copy(out_weight_hbm, mine, local_sem.at[6])
@@ -209,6 +206,19 @@
     ]
     for copy in weight_copies:
         copy.start()
+    if gather:
+        weight_twin = remote(out_weight_hbm, mine, g_sem.at[0], g_sem.at[1], twin)
+        weight_forward = [
+            pltpu.make_async_remote_copy(
+                src_ref=theirs,
+                dst_ref=theirs,
+                send_sem=w_send.at[len(far) + k],
+                recv_sem=w_recv.at[len(far) + k],
+                device_id=device,
+                device_id_type=MESH,
+            )
+            for k, device in enumerate(far)
+        ]
 
     bias = bias_ref[:, cols(me, 3 * width)]
     low = lax.broadcasted_iota(jnp.int32, (rows, 128), 1) < HEAD_DIM
@@ -237,6 +247,9 @@
     project(me)
     to_partner.wait_recv()
     project(partner)
+    to_twin.wait_send()
+    if gather:
+        weight_twin.start()
     to_twin.wait_recv()
     forward.start()
     project(twin)
@@ -255,128 +268,134 @@
 
     blocks = tok.shape[0]
     new_rows = blocks * rows
-    for block in range(blocks):
-        seen = (block + 1) * rows
-        stacked_row = lax.broadcasted_iota(jnp.int32, (heads * rows, seen), 0) % rows
-        new = lax.broadcasted_iota(jnp.int32, (heads * rows, seen), 1)
-        alive = (new <= block * rows + stacked_row) & (new < filled)
-        new_cap = jnp.where(alive, LIVE, DEAD)
-        numer, top, total = attend(
-            qo[block],
-            [kc[0, 0], kc[0, 1], kn[0 : block + 1].reshape(seen, width)],
-            caps + [new_cap],
-            [vc[0, 0], vc[0, 1], vn[0 : block + 1].reshape(seen, width)],
-            heads,
+    new = lax.broadcasted_iota(jnp.int32, (heads * rows, new_rows), 1)
+    stacked_row = lax.broadcasted_iota(jnp.int32, (heads * rows, new_rows), 0) % rows
+
+    def part_copies(group, slot):
+        return (
+            remote(
+                part_send.at[group, slot],
+                part_recv.at[1 - group, slot],
+                p_send.at[0, group, slot],
+                p_recv.at[0, 1 - group, slot],
+                twin,
+            ),
+            remote(
+                stat_send.at[group, slot],
+                stat_recv.at[1 - group, slot],
+                p_send.at[1, group, slot],
+                p_recv.at[1, 1 - group, slot],
+                twin,
+            ),
         )
-        numer_own[block] = pick(numer, rows, heads)
-        stat_own[block] = stat_tile(top, total, rows, heads)
+
+    def partial(group, local_rows):
+        def body(slot, carry):
+            base = chip if local_rows else 1 - chip
+            block = 2 * base + (core + slot) % 2
+            if group == 0:
+                alive = (new <= block * rows + stacked_row) & (new < filled)
+                numer, top, total = attend(
+                    qo[block],
+                    [kc[0, 0], kc[0, 1], kn[...].reshape(new_rows, width)],
+                    caps + [jnp.where(alive, LIVE, DEAD)],
+                    [vc[0, 0], vc[0, 1], vn[...].reshape(new_rows, width)],
+                    heads,
+                )
+            else:
+                query_copy(block).wait_recv()
+                numer, top, total = attend(
+                    qt[block], [kc[1, 0], kc[1, 1]], caps, [vc[1, 0], vc[1, 1]], heads
+                )
+            stats = stat_tile(top, total, rows, heads)
+            if local_rows:
+                numer_keep[group, slot] = pick(numer, rows, heads)
+                stat_keep[group, slot] = stats
+            else:
+                part_send[group, slot] = pick(numer / total, rows, heads).astype(BF16)
+                stat_send[group, slot] = stats.T[0 : 2 * heads]
+                for copy in part_copies(group, slot):
+                    copy.start()
+            return carry
+
+        lax.fori_loop(0, 2, body, 0)
+
+    def combine(group, slot):
+        for copy in part_copies(1 - group, slot):
+            copy.wait_recv()
+        other = jnp.concatenate(
+            [stat_recv[group, slot], jnp.ones((rows - 2 * heads, rows), F32)], 0
+        ).T
+        own = stat_keep[group, slot]
+        best = jnp.maximum(own, other)
+        scale_own = pltpu.roll(own, 128 - heads, 1) * jnp.exp(own - best)
+        scale_other = pltpu.roll(other, 128 - heads, 1) * jnp.exp(other - best)
+        denom = scale_own + scale_other
+        first = jnp.exp(own - best) / denom
+        mixed = numer_keep[group, slot] * spread(first, rows, heads)
+        mixed = mixed + part_recv[group, slot].astype(F32) * spread(
+            scale_other / denom, rows, heads
+        )
+        attn[slot, group] = mixed.astype(BF16)
+
+    partial(0, False)
+    if gather:
+        weight_twin.wait_recv()
+        for copy in weight_forward:
+            copy.start()
+    partial(1, False)
+    partial(0, True)
+    partial(1, True)
 
     own_weight.wait()
     for copy in weight_copies:
         copy.wait_recv()
-    share_weight = remote(wo, other_wo, f_sem.at[0], f_sem.at[1], partner)
-    share_weight.start()
-
-    def part_copies(block):
-        return (
-            remote(
-                part_send.at[block],
-                part_recv.at[block],
-                p_send.at[0, block],
-                p_recv.at[0, block],
-                twin,
-            ),
-            remote(
-                stat_send.at[block],
-                stat_recv.at[block],
-                p_send.at[1, block],
-                p_recv.at[1, block],
-                twin,
-            ),
-        )
-
-    def twin_block(step, carry):
-        block = 2 * ((chip + step // 2) % 2) + (core + step // 2 + step + 1) % 2
-        query_copy(block).wait_recv()
-        numer, top, total = attend(
-            qt[block], [kc[1, 0], kc[1, 1]], caps, [vc[1, 0], vc[1, 1]], heads
-        )
-        part_send[block] = pick(numer / total, rows, heads).astype(BF16)
-        stat_send[block] = stat_tile(top, total, rows, heads).T[0 : 2 * heads]
-        for copy in part_copies(block):
-            copy.start()
-        return carry
-
-    def combine(block):
-        for copy in part_copies(block):
+    late = []
+    if gather:
+        for copy in weight_forward:
             copy.wait_recv()
-        other = jnp.concatenate(
-            [stat_recv[block], jnp.ones((rows - 2 * heads, rows), F32)], 0
-        ).T
-        own = stat_own[block]
-        best = jnp.maximum(own, other)
-        scale_own = jnp.exp(own - best)
-        scale_other = pltpu.roll(other, 128 - heads, 1) * jnp.exp(other - best)
-        denom = pltpu.roll(own, 128 - heads, 1) * scale_own + scale_other
-        mixed = numer_own[block] * spread(scale_own / denom, rows, heads)
-        mixed = mixed + part_recv[block].astype(F32) * spread(scale_other / denom, rows, heads)
-        attn[block] = mixed.astype(BF16)
-
-    shared = [
-        remote(attn.at[owner], other_attn.at[at], a_send.at[at], a_recv.at[at], partner)
-        for at, owner in enumerate((partner, diag))
-    ]
-    pieces, _, span = y_send.shape
-
-    def product(block, at, piece):
-        here = slice(piece * span, (piece + 1) * span)
-        return jnp.dot(attn[block], wo[:, here], preferred_element_type=F32) + jnp.dot(
-            other_attn[at], other_wo[:, here], preferred_element_type=F32
-        )
-
-    y_copies = [
-        remote(y_send.at[i], y_recv.at[i], ys_sem.at[i], yr_sem.at[i], twin)
-        for i in range(pieces)
-    ]
-
-    lax.fori_loop(0, blocks - 1, twin_block, 0)
-    combine(diag)
-    shared[1].start()
-    combine(twin)
-    twin_block(blocks - 1, 0)
-    share_weight.wait_recv()
-    shared[1].wait_recv()
-    for i in range(pieces):
-        y_send[i] = product(twin, 1, i).astype(BF16)
-        y_copies[i].start()
-    combine(partner)
-    shared[0].start()
-    combine(me)
-    shared[0].wait_recv()
-    mixed = [product(me, 0, i) for i in range(pieces)]
-    for i in range(pieces):
-        y_copies[i].wait_recv()
-    mixed = jnp.concatenate(
-        [mixed[i] + y_recv[i].astype(F32) for i in range(pieces)], 1
-    )
+        late = [
+            remote(wo.at[owner], wo.at[owner], f_sem.at[0, at], f_sem.at[1, at], partner)
+            for at, owner in enumerate((me, twin))
+        ]
+    for copy in late:
+        copy.start()
+
+    shared = remote(attn.at[1], other_attn, a_send.at[0], a_recv.at[0], partner)
+    combine(0, 1)
+    combine(1, 1)
+    shared.start()
+    combine(0, 0)
+    combine(1, 0)
+    mixed = jnp.dot(attn[0, 0], wo[me], preferred_element_type=F32)
+    mixed = mixed + jnp.dot(attn[0, 1], wo[twin], preferred_element_type=F32)
+    for copy in late:
+        copy.wait_recv()
+    shared.wait_recv()
+    mixed = mixed + jnp.dot(other_attn[0], wo[partner], preferred_element_type=F32)
+    mixed = mixed + jnp.dot(other_attn[1], wo[diag], preferred_element_type=F32)
     mixed = mixed + out_bias_ref[...] + tok[me].astype(F32)
     center = mixed - jnp.mean(mixed, axis=1, keepdims=True)
     variance = jnp.mean(center * center, axis=1, keepdims=True)
     normed = center * lax.rsqrt(variance + 1e-05) * gain_ref[...] + shift_ref[...]
     out_ref[0] = normed.astype(BF16)
 
-    for copy in [to_twin, to_partner, forward, share_weight]:
-        copy.wait_send()
-    for copy in cache_copies + weight_copies + shared + y_copies:
+    late.append(shared)
+    if gather:
+        late.append(weight_twin)
+        late.extend(weight_forward)
+    for copy in [to_partner, forward] + late + cache_copies + weight_copies:
         copy.wait_send()
 
     def drain(block, carry):
         query_copy(block).wait_send()
-        for copy in part_copies(block):
-            copy.wait_send()
         return carry
 
     lax.fori_loop(0, blocks, drain, 0)
+    for group in range(2):
+        for slot in range(2):
+            for copy in part_copies(group, slot):
+                copy.wait_send()
 
 
 def local(
@@ -406,8 +425,8 @@
     gather = out_weight.shape[1] % 128 == 0
     if not gather:
         out_weight = lax.all_gather(out_weight, "dp", axis=1, tiled=True)
+        out_weight = lax.all_gather(out_weight, "seq", axis=0)
     far = lax.axis_size("dp") - 1 if gather else 1
-    pieces = 4
 
     def half(count):
         return pltpu.VMEM((count, rows, width), BF16)
@@ -426,18 +445,15 @@
             half(blocks),
             half(blocks),
             half(blocks),
-            pltpu.VMEM((blocks, rows, width), F32),
-            pltpu.VMEM((blocks, rows, 128), F32),
-            half(blocks),
-            half(blocks),
-            pltpu.VMEM((blocks, 2 * heads, rows), F32),
-            pltpu.VMEM((blocks, 2 * heads, rows), F32),
-            half(blocks),
+            pltpu.VMEM((2, 2, rows, width), F32),
+            pltpu.VMEM((2, 2, rows, 128), F32),
+            pltpu.VMEM((2, 2, rows, width), BF16),
+            pltpu.VMEM((2, 2, rows, width), BF16),
+            pltpu.VMEM((2, 2, 2 * heads, rows), F32),
+            pltpu.VMEM((2, 2, 2 * heads, rows), F32),
+            pltpu.VMEM((2, 2, rows, width), BF16),
             half(2),
-            pltpu.VMEM((width, model), BF16),
-            pltpu.VMEM((width, model), BF16),
-            pltpu.VMEM((pieces, rows, model // pieces), BF16),
-            pltpu.VMEM((pieces, rows, model // pieces), BF16),
+            pltpu.VMEM((blocks, width, model), BF16),
             dma((7,)),
             dma((3,)),
             dma((3,)),
@@ -445,15 +461,14 @@
             dma((4,)),
             dma((blocks,)),
             dma((blocks,)),
-            dma((2, blocks)),
-            dma((2, blocks)),
+            dma((2, 2, 2)),
+            dma((2, 2, 2)),
+            dma((1,)),
+            dma((1,)),
+            dma((2 * far,)),
+            dma((2 * far,)),
+            dma((2, 2)),
             dma((2,)),
-            dma((2,)),
-            dma((far,)),
-            dma((far,)),
-            dma((2,)),
-            dma((pieces,)),
-            dma((pieces,)),
         ],
         compiler_params=pltpu.CompilerParams(
             collective_id=0, has_side_effects=True, vmem_limit_bytes=60 << 20

time: 42.6 us -> 38.9 us (0.913)
  Pallas kernels: 40.7 us -> 37 us
    pallas_call x1, Pallas kernels: 40.7 us -> 37 us  [local(): pl.pallas_call(functools.partial(kernel, gather), out_shape=jax.ShapeDtyp...]
where the time goes in v3:
time: 38.9 us; the launch traced here: 38.6 us
  Pallas kernels  37 us (95%)
  local copies, waits for them, and re-layouts  1.67 us (4%)
    pallas_call x1, Pallas kernels, local(): pl.pallas_call(functools.partial(kernel, gather), out_shape=jax.ShapeDtyp...  37 us
    unnamed x1, local copies, waits for them, and re-layouts  1.67 us

profile of v3, /device:TPU:0, one launch (start us, length us, event | category | flops | bytes accessed | tf_op | source)
XLA Modules:
  0.0 38.6 jit_solution(5349258697134903005)
XLA Ops:
  0.0 37.0 %sublayer.1 = bf16[1,128,1024]{2,1,0:T(8,128)(2,1)} custom-call(s32[8]{0:T(128)} %cached_ref.1, s32[8]{0:T(128)} %span_ref.1, s32[8]{0:T(128)} %slot_ref.1, bf16[1,128,1024]{2,1,0:T(8,128)(2,1)} %tokens_hbm.1, bf16[1,512,1024]{2,1,0:T(8,128)(2,1)} %keys_hbm.1, bf16[1,512,1024]{2,1,0:T(8,128)(2,1)} %values_hbm.1, bf16[1024,768]{1,0:T(8,128)(2,1)} %weight_hbm.1, ...), custom_call_target="tpu_custom_call" | custom-call | flops 6000000000 | bytes 6000000 | tf_op jit(solution)/shard_map/sublayer/pallas_call | solution.py:434
  37.0 1.7 %copy.14 = bf16[1,128,1024]{2,1,0:T(8,128)(2,1)} copy(bf16[1,128,1024]{2,1,0:T(8,128)(2,1)} %sublayer.1) | data formatting | bytes 524288

commit v4 on v3

--- a/solution.py
+++ b/solution.py
@@ -32,7 +32,7 @@
     return lax.dot_general(a, b, (((1,), (1,)), ((), ())), preferred_element_type=F32)
 
 
-def attend(query, keys, caps, values, heads):
+def attend(query, keys, caps, values, heads, before=None):
     rows, width = query.shape
     lane = lax.broadcasted_iota(jnp.int32, (rows, width), 1) // HEAD_DIM
     zero = jnp.zeros_like(query)
@@ -40,6 +40,10 @@
     scores = [jnp.minimum(nt(stacked, k), cap) for k, cap in zip(keys, caps)]
     top = functools.reduce(jnp.maximum, [jnp.max(s, 1, keepdims=True) for s in scores])
     total, numer = 0.0, 0.0
+    if before is not None:
+        top = jnp.maximum(top, before[1])
+        fade = jnp.exp(before[1] - top)
+        numer, total = before[0] * fade, before[2] * fade
     for s, v in zip(scores, values):
         weights = jnp.exp(s - top)
         total = total + jnp.sum(weights, 1, keepdims=True)
@@ -98,6 +102,8 @@
     qt,
     numer_keep,
     stat_keep,
+    early_numer,
+    early_stat,
     part_send,
     part_recv,
     stat_send,
@@ -250,21 +256,32 @@
     to_twin.wait_send()
     if gather:
         weight_twin.start()
+
+    for copy in locals_[2:]:
+        copy.wait()
+    for copy in cache_copies:
+        copy.wait_recv()
+    place = lax.broadcasted_iota(jnp.int32, (1, cache_rows), 1)
+    caps = [
+        jnp.where((2 * chip + j) * cache_rows + place < cached, LIVE, DEAD) for j in range(2)
+    ]
+
+    def early(slot, carry):
+        block = 2 * chip + (core + slot) % 2
+        numer, top, total = attend(
+            qo[block], [kc[0, 0], kc[0, 1]], caps, [vc[0, 0], vc[0, 1]], heads
+        )
+        early_numer[slot] = numer
+        early_stat[slot, 0] = top
+        early_stat[slot, 1] = total
+        return carry
+
+    lax.fori_loop(0, 2, early, 0)
     to_twin.wait_recv()
     forward.start()
     project(twin)
     forward.wait_recv()
     project(diag)
-
-    for copy in locals_[2:]:
-        copy.wait()
-    for copy in cache_copies:
-        copy.wait_recv()
-
-    place = lax.broadcasted_iota(jnp.int32, (1, cache_rows), 1)
-    caps = [
-        jnp.where((2 * chip + j) * cache_rows + place < cached, LIVE, DEAD) for j in range(2)
-    ]
 
     blocks = tok.shape[0]
     new_rows = blocks * rows
@@ -295,13 +312,17 @@
             block = 2 * base + (core + slot) % 2
             if group == 0:
                 alive = (new <= block * rows + stacked_row) & (new < filled)
-                numer, top, total = attend(
-                    qo[block],
-                    [kc[0, 0], kc[0, 1], kn[...].reshape(new_rows, width)],
-                    caps + [jnp.where(alive, LIVE, DEAD)],
-                    [vc[0, 0], vc[0, 1], vn[...].reshape(new_rows, width)],
-                    heads,
-                )
+                keys = [kn[...].reshape(new_rows, width)]
+                values = [vn[...].reshape(new_rows, width)]
+                limits = [jnp.where(alive, LIVE, DEAD)]
+                before = None
+                if local_rows:
+                    before = (early_numer[slot], early_stat[slot, 0], early_stat[slot, 1])
+                else:
+                    keys = [kc[0, 0], kc[0, 1]] + keys
+                    values = [vc[0, 0], vc[0, 1]] + values
+                    limits = caps + limits
+                numer, top, total = attend(qo[block], keys, limits, values, heads, before)
             else:
                 query_copy(block).wait_recv()
                 numer, top, total = attend(
@@ -312,7 +333,7 @@
                 numer_keep[group, slot] = pick(numer, rows, heads)
                 stat_keep[group, slot] = stats
             else:
-                part_send[group, slot] = pick(numer / total, rows, heads).astype(BF16)
+                part_send[group, slot] = pick(numer * (1.0 / total), rows, heads).astype(BF16)
                 stat_send[group, slot] = stats.T[0 : 2 * heads]
                 for copy in part_copies(group, slot):
                     copy.start()
@@ -447,6 +468,8 @@
             half(blocks),
             pltpu.VMEM((2, 2, rows, width), F32),
             pltpu.VMEM((2, 2, rows, 128), F32),
+            pltpu.VMEM((2, heads * rows, width), F32),
+            pltpu.VMEM((2, 2, heads * rows, 1), F32),
             pltpu.VMEM((2, 2, rows, width), BF16),
             pltpu.VMEM((2, 2, rows, width), BF16),
             pltpu.VMEM((2, 2, 2 * heads, rows), F32),

time: 38.9 us -> 40 us (1.028)
  the two profiles are of different devices: /device:TPU:0 before, /device:TPU:15 now
where the time goes in v4:
time: 40 us; the launch traced here: 39.8 us
  Pallas kernels  38.1 us (95%)
  local copies, waits for them, and re-layouts  1.67 us (4%)
    pallas_call x1, Pallas kernels, local(): pl.pallas_call(functools.partial(kernel, gather), out_shape=jax.ShapeDtyp...  38.1 us
    unnamed x1, local copies, waits for them, and re-layouts  1.67 us

profile of v4, /device:TPU:15, one launch (start us, length us, event | category | flops | bytes accessed | tf_op | source)
XLA Modules:
  0.0 39.8 jit_solution(8344817175942354572)
XLA Ops:
  0.0 38.1 %sublayer.1 = bf16[1,128,1024]{2,1,0:T(8,128)(2,1)} custom-call(s32[8]{0:T(128)} %cached_ref.1, s32[8]{0:T(128)} %span_ref.1, s32[8]{0:T(128)} %slot_ref.1, bf16[1,128,1024]{2,1,0:T(8,128)(2,1)} %tokens_hbm.1, bf16[1,512,1024]{2,1,0:T(8,128)(2,1)} %keys_hbm.1, bf16[1,512,1024]{2,1,0:T(8,128)(2,1)} %values_hbm.1, bf16[1024,768]{1,0:T(8,128)(2,1)} %weight_hbm.1, ...), custom_call_target="tpu_custom_call" | custom-call | flops 6000000000 | bytes 6000000 | tf_op jit(solution)/shard_map/sublayer/pallas_call | solution.py:455
  38.1 1.7 %copy.14 = bf16[1,128,1024]{2,1,0:T(8,128)(2,1)} copy(bf16[1,128,1024]{2,1,0:T(8,128)(2,1)} %sublayer.1) | data formatting | bytes 524288

commit v5 on v3

--- a/solution.py
+++ b/solution.py
@@ -270,6 +270,7 @@
     new_rows = blocks * rows
     new = lax.broadcasted_iota(jnp.int32, (heads * rows, new_rows), 1)
     stacked_row = lax.broadcasted_iota(jnp.int32, (heads * rows, new_rows), 0) % rows
+    ahead = jnp.where(new < filled, new - stacked_row, 2 * new_rows)
 
     def part_copies(group, slot):
         return (
@@ -294,7 +295,7 @@
             base = chip if local_rows else 1 - chip
             block = 2 * base + (core + slot) % 2
             if group == 0:
-                alive = (new <= block * rows + stacked_row) & (new < filled)
+                alive = ahead <= block * rows
                 numer, top, total = attend(
                     qo[block],
                     [kc[0, 0], kc[0, 1], kn[...].reshape(new_rows, width)],
@@ -312,7 +313,7 @@
                 numer_keep[group, slot] = pick(numer, rows, heads)
                 stat_keep[group, slot] = stats
             else:
-                part_send[group, slot] = pick(numer / total, rows, heads).astype(BF16)
+                part_send[group, slot] = pick(numer * (1.0 / total), rows, heads).astype(BF16)
                 stat_send[group, slot] = stats.T[0 : 2 * heads]
                 for copy in part_copies(group, slot):
                     copy.start()

time: 38.9 us -> 39 us (level)
  no operation moved by 1% of the time
where the time goes in v5:
time: 39 us; the launch traced here: 38.6 us
  Pallas kernels  37 us (95%)
  local copies, waits for them, and re-layouts  1.67 us (4%)
    pallas_call x1, Pallas kernels, local(): pl.pallas_call(functools.partial(kernel, gather), out_shape=jax.ShapeDtyp...  37 us
    unnamed x1, local copies, waits for them, and re-layouts  1.67 us

profile of v5, /device:TPU:0, one launch (start us, length us, event | category | flops | bytes accessed | tf_op | source)
XLA Modules:
  0.0 38.6 jit_solution(4559598808331255485)
XLA Ops:
  0.0 37.0 %sublayer.1 = bf16[1,128,1024]{2,1,0:T(8,128)(2,1)} custom-call(s32[8]{0:T(128)} %cached_ref.1, s32[8]{0:T(128)} %span_ref.1, s32[8]{0:T(128)} %slot_ref.1, bf16[1,128,1024]{2,1,0:T(8,128)(2,1)} %tokens_hbm.1, bf16[1,512,1024]{2,1,0:T(8,128)(2,1)} %keys_hbm.1, bf16[1,512,1024]{2,1,0:T(8,128)(2,1)} %values_hbm.1, bf16[1024,768]{1,0:T(8,128)(2,1)} %weight_hbm.1, ...), custom_call_target="tpu_custom_call" | custom-call | flops 6000000000 | bytes 6000000 | tf_op jit(solution)/shard_map/sublayer/pallas_call | solution.py:435
  37.0 1.7 %copy.14 = bf16[1,128,1024]{2,1,0:T(8,128)(2,1)} copy(bf16[1,128,1024]{2,1,0:T(8,128)(2,1)} %sublayer.1) | data formatting | bytes 524288
